TPU v7x, 32 devices: a whole 2x2x4 slice. The times are simulated.
32 devices in a mesh: group: 2 (over x), col: 16 (over z, y, core).
Axes of the slice: x: 2, y: 2, z: 4, core: 2. Of those that a mesh axis runs over, the one named last changes fastest.
Arguments:
- homolog_embedding: bfloat16 [192, 64, 256], P('group', 'col'), parts along dimension 0, may hold values from -6 to 6
- left_factor_matrix: bfloat16 [256, 32], replicated, may hold values from -0.375 to 0.375
- right_factor_matrix: bfloat16 [256, 32], replicated, may hold values from -0.375 to 0.375
- decoder: bfloat16 [1024, 128], replicated, may hold values from -2 to 2
- pair_output_bias: float32 [128], replicated, may hold values from -3 to 3
- pair_output_gradient: bfloat16 [128, 64, 128], P('group', 'col'), parts along dimension 0, may hold values from -6 to 6
Outputs:
- first_operand_gradient: float32 [192, 64, 32], P('group', 'col'), parts along dimension 0
- second_operand_gradient: float32 [192, 64, 32], P('group', 'col'), parts along dimension 0
- alignment_gradient: bfloat16 [192, 64, 256], P('group', 'col'), parts along dimension 0
There are 2 independent parts, one for each index of `group`. A program takes and returns all parts, laid end to end along the dimension named above; an argument that names none is the same for every part. Nothing has to cross between parts.
All inputs are finite; a program needn't handle non-finite values.
Results may differ from a plain program's by a relative error of at most 0.0083.
Values may be sent and summed in bfloat16 or wider, within the bound.
A program may use at most 64 MiB of HBM per device.

v0:
```python
import jax
import jax.numpy as jnp
from jax import lax
from jax.sharding import PartitionSpec as P


def per_device(
    homolog_embedding,
    left_factor_matrix,
    right_factor_matrix,
    decoder,
    pair_output_bias,
    pair_output_gradient,
):
    alignment_row_count, local_residue_start, alignment_channel_width = homolog_embedding.shape
    operand_channel_width = left_factor_matrix.shape[1]
    channels = decoder.shape[1]
    residue_total_count = local_residue_start * lax.axis_size("col")
    reciprocal_rows = 1.0 / alignment_row_count
    block_res = local_residue_start * max(1, 96 // local_residue_start)
    alignment_flattened_rows = homolog_embedding.reshape(
        alignment_row_count * local_residue_start, alignment_channel_width
    )
    first_operand_rows = (
        jnp.dot(alignment_flattened_rows, left_factor_matrix, preferred_element_type=jnp.float32)
        .astype(jnp.bfloat16)
        .reshape(alignment_row_count, local_residue_start * operand_channel_width)
    )
    second_operand_rows = (
        jnp.dot(alignment_flattened_rows, right_factor_matrix, preferred_element_type=jnp.float32)
        .astype(jnp.bfloat16)
        .reshape(alignment_row_count, local_residue_start * operand_channel_width)
    )
    second_operand_local = second_operand_rows.reshape(
        alignment_row_count, local_residue_start, operand_channel_width
    )

    def outer_slopes(slope_rows, rows_by_length, col_span):
        backward = (
            jnp.dot(slope_rows, decoder.T, preferred_element_type=jnp.float32) * reciprocal_rows
        )
        return backward.astype(jnp.bfloat16).reshape(
            rows_by_length, col_span, operand_channel_width, operand_channel_width
        )

    offset_col = jnp.int32(0)
    second_operand_gradient = jnp.zeros(
        (alignment_row_count, local_residue_start, operand_channel_width), jnp.float32
    )
    stored = jnp.zeros((residue_total_count, local_residue_start * channels), jnp.bfloat16)
    left_segment = lax.all_gather(first_operand_rows, "col", axis=1, tiled=True)
    right_segment = lax.all_gather(second_operand_rows, "col", axis=1, tiled=True)
    right_whole = right_segment
    piece_res = left_segment.shape[1] // operand_channel_width
    first_res = offset_col // operand_channel_width
    collected = []
    for split_offset in range(0, piece_res, block_res):
        split_rows_by_length = min(block_res, piece_res - split_offset)
        split_left_block = left_segment[
            :,
            split_offset
            * operand_channel_width : (split_offset + split_rows_by_length)
            * operand_channel_width,
        ].reshape(alignment_row_count, split_rows_by_length, operand_channel_width)
        collected.append((split_rows_by_length, split_left_block, first_res + split_offset))
    for rows_by_length, left_block, first_row in collected:
        products = (
            jnp.einsum(
                "sic,sjd->ijcd",
                left_block,
                second_operand_local,
                preferred_element_type=jnp.float32,
            )
            * reciprocal_rows
        )
        products = products.astype(jnp.bfloat16).reshape(
            rows_by_length * local_residue_start, operand_channel_width * operand_channel_width
        )
        linear = jnp.dot(products, decoder, preferred_element_type=jnp.float32) + pair_output_bias
        upstream = lax.dynamic_slice_in_dim(pair_output_gradient, first_row, rows_by_length, 0)
        upstream = upstream.reshape(rows_by_length * local_residue_start, channels).astype(
            jnp.float32
        )
        accumulate_slope_rows = (upstream * 2.0 * jnp.maximum(linear, 0.0)).astype(jnp.bfloat16)
        stored = lax.dynamic_update_slice_in_dim(
            stored,
            accumulate_slope_rows.reshape(rows_by_length, local_residue_start * channels),
            first_row,
            0,
        )
        accumulate_slopes = outer_slopes(accumulate_slope_rows, rows_by_length, local_residue_start)
        second_operand_gradient = second_operand_gradient + jnp.einsum(
            "ijcd,sic->sjd", accumulate_slopes, left_block, preferred_element_type=jnp.float32
        )
    second_operand_gradient, stored, right_whole = (second_operand_gradient, stored, right_whole)
    received = lax.all_to_all(stored, "col", split_axis=0, concat_axis=1, tiled=True)
    right_all = right_whole.reshape(alignment_row_count, residue_total_count, operand_channel_width)
    col_span = local_residue_start * max(
        max(1, 96 // local_residue_start), lax.axis_size("col") // 8
    )
    first_operand_gradient = jnp.zeros(
        (alignment_row_count, local_residue_start, operand_channel_width), jnp.float32
    )
    for offset in range(0, residue_total_count, col_span):
        width_cols = min(col_span, residue_total_count - offset)
        slope_rows = received[:, offset * channels : (offset + width_cols) * channels].reshape(
            local_residue_start * width_cols, channels
        )
        slopes = outer_slopes(slope_rows, local_residue_start, width_cols)
        first_operand_gradient = first_operand_gradient + jnp.einsum(
            "ijcd,sjd->sic",
            slopes,
            right_all[:, offset : offset + width_cols],
            preferred_element_type=jnp.float32,
        )
    first_operand_gradient_step = first_operand_gradient.astype(jnp.bfloat16).reshape(
        alignment_row_count * local_residue_start, operand_channel_width
    )
    second_operand_gradient_step = second_operand_gradient.astype(jnp.bfloat16).reshape(
        alignment_row_count * local_residue_start, operand_channel_width
    )
    alignment_gradient = jnp.dot(
        first_operand_gradient_step, left_factor_matrix.T, preferred_element_type=jnp.float32
    ) + jnp.dot(
        second_operand_gradient_step, right_factor_matrix.T, preferred_element_type=jnp.float32
    )
    alignment_gradient = alignment_gradient.astype(jnp.bfloat16).reshape(
        alignment_row_count, local_residue_start, alignment_channel_width
    )
    return (first_operand_gradient, second_operand_gradient, alignment_gradient)


def solution(mesh):
    placed = (P("group", "col", None), P(), P(), P(), P(), P("group", "col", None))
    return jax.shard_map(
        per_device,
        mesh=mesh,
        in_specs=placed,
        out_specs=(P("group", "col", None), P("group", "col", None), P("group", "col", None)),
        check_vma=False,
    )
```

profile of v0, /device:TPU:0, one launch (start us, length us, event | category | flops | bytes accessed | tf_op | source)
XLA Modules:
  0.0 74.2 jit_solution(9161705522396213601)
XLA Ops:
  0.6 0.0 copy-start
  0.7 1.0 %reshape.53 = bf16[384,256]{1,0:T(8,128)(2,1)S(1)} reshape(bf16[96,4,256]{2,1,0:T(4,128)(2,1)} %param.6) | data formatting | bytes 393216 | tf_op jit(solution)/shard_map/reshape | solution.py:21
  1.7 0.9 %convolution_convert_fusion = bf16[384,32]{0,1:T(8,128)(2,1)S(1)} fusion(bf16[384,256]{1,0:T(8,128)(2,1)S(1)} %reshape.53, bf16[256,32]{0,1:T(8,128)(2,1)} %param.7), kind=kOutput, calls=%fused_computation.14 | convolution fusion | flops 6303744 | bytes 237568 | tf_op jit(solution)/shard_map/dot_general | solution.py:25
  2.6 0.1 copy.31
  2.7 0.1 reshape.56
  2.8 24.2 %all_gather.7 = bf16[96,2048]{1,0:T(8,128)(2,1)S(1)} all-gather(bf16[96,128]{1,0:T(8,128)(2,1)S(1)} %reshape.56), channel_id=1, replica_groups=mesh['group'=2,'col'=16] {'col'}, dimensions={1}, use_global_device_ids=true | all-gather | bytes 417792 | tf_op jit(solution)/shard_map/all_gather | solution.py:51
  27.0 0.3 copy.32
  27.3 0.2 convolution_convert_fusion.1
  27.5 0.1 copy.28
  27.6 1.6 %fusion = bf16[64,4,32,32]{0,3,2,1:T(8,128)(2,1)} fusion(bf16[96,64,32]{0,2,1:T(8,128)(2,1)S(1)} %bitcast.48, bf16[96,4,32,1]{2,1,0,3:T(4,128)(2,1)S(1)} %bitcast.51), kind=kOutput, calls=%fused_computation.1 | convolution fusion | flops 50855936 | bytes 942080 | tf_op jit(solution)/shard_map/sic,sjd->ijcd/dot_general | solution.py:68
  29.3 4.2 %copy.35 = bf16[64,4,32,32]{3,2,1,0:T(8,128)(2,1)S(1)} copy(bf16[64,4,32,32]{0,3,2,1:T(8,128)(2,1)} %fusion) | data formatting | bytes 1048576 | tf_op jit(solution)/shard_map/convert_element_type | solution.py:76
  33.5 2.2 %reshape.58 = bf16[256,1024]{1,0:T(8,128)(2,1)S(1)} reshape(bf16[64,4,32,32]{3,2,1,0:T(8,128)(2,1)S(1)} %copy.35) | data formatting | bytes 1048576 | tf_op jit(solution)/shard_map/reshape | solution.py:76
  35.7 0.9 %convert_multiply_fusion = f32[64,4,128]{2,1,0:T(4,128)S(1)} fusion(bf16[64,4,128]{2,1,0:T(4,128)(2,1)} %param.11), kind=kLoop, calls=%fused_computation.18 | loop fusion | flops 65536 | bytes 196608 | tf_op jit(solution)/shard_map/mul | solution.py:84
  36.6 0.3 fusion.6
  36.9 0.7 all_to_all.12
  37.6 4.2 %all-to-all-start = ((bf16[16,4,512]{2,1,0:T(4,128)(2,1)}), bf16[16,4,512]{2,1,0:T(4,128)(2,1)}, u32[]{:S(2)}, u32[]{:S(2)}) async-start(bf16[16,4,512]{2,1,0:T(4,128)(2,1)} %all_to_all.12), calls=%async_computation | async-start | bytes 131072 | tf_op jit(solution)/shard_map/all_to_all | solution.py:96
  41.7 0.7 reshape.54
  42.5 0.3 fusion.2
  42.8 1.6 %reshape.61 = bf16[64,4,32,32]{3,2,1,0:T(8,128)(2,1)S(1)} reshape(bf16[256,1024]{1,0:T(8,128)(2,1)S(1)} %fusion.2) | data formatting | bytes 1048576 | tf_op jit(solution)/shard_map/reshape | solution.py:42
  44.4 1.3 %fusion.11 = (bf16[96,4,32]{0,2,1:T(8,128)(2,1)S(1)}, f32[96,4,32]{0,2,1:T(8,128)}) fusion(bf16[96,64,32,1]{0,2,3,1:T(8,128)(2,1)S(1)} %bitcast.49, bf16[64,4,32,32]{3,2,1,0:T(8,128)(2,1)S(1)} %reshape.61), kind=kOutput, calls=%fused_computation.21 | convolution fusion | flops 50343936 | bytes 991232 | tf_op jit(solution)/shard_map/ijcd,sic->sjd/dot_general | solution.py:92
  45.7 22.7 %all_gather.6 = bf16[96,2048]{1,0:T(8,128)(2,1)S(1)} all-gather(bf16[96,128]{1,0:T(8,128)(2,1)S(1)} %copy-done.1), channel_id=1, replica_groups=mesh['group'=2,'col'=16] {'col'}, dimensions={1}, use_global_device_ids=true | all-gather | bytes 417792 | tf_op jit(solution)/shard_map/all_gather | solution.py:52
  68.4 0.3 copy.29
  68.7 0.1 copy.41
  68.8 0.9 %copy.36 = bf16[4,16,512]{2,1,0:T(8,128)(2,1)S(1)} copy(bf16[4,16,512]{2,0,1:T(4,128)(2,1)} %bitcast.8) | data formatting | bytes 131072 | tf_op jit(solution)/shard_map/all_to_all | solution.py:96
  69.7 0.1 reshape.59
  69.7 0.3 fusion.1
  70.0 1.6 %reshape.71 = bf16[4,64,32,32]{3,2,1,0:T(8,128)(2,1)S(1)} reshape(bf16[256,1024]{1,0:T(8,128)(2,1)S(1)} %fusion.1) | data formatting | bytes 1048576 | tf_op jit(solution)/shard_map/reshape | solution.py:42
  71.6 1.3 %fusion.10 = (bf16[96,4,32]{0,2,1:T(8,128)(2,1)S(1)}, f32[96,4,32]{0,2,1:T(8,128)}) fusion(bf16[96,64,32,1]{0,2,1,3:T(8,128)(2,1)S(1)} %bitcast.50, bf16[4,64,32,32]{3,2,1,0:T(8,128)(2,1)S(1)} %reshape.71), kind=kOutput, calls=%fused_computation.20 | convolution fusion | flops 50343936 | bytes 991232 | tf_op jit(solution)/shard_map/ijcd,sjd->sic/dot_general | solution.py:110
  73.0 0.1 copy.40
  73.1 0.2 fusion.12
  73.3 0.2 fusion.3
  73.5 0.7 reshape.64
  (10 shorter events, 0.0 us)
Async XLA Ops:
  0.6 36.0 %copy-start = (bf16[1024,128]{1,0:T(8,128)(2,1)S(1)}, bf16[1024,128]{1,0:T(8,128)(2,1)}, u32[]{:S(2)}) copy-start(bf16[1024,128]{1,0:T(8,128)(2,1)} %param.9) | copy-start | bytes 786436
  0.6 26.7 %copy-start.3 = (bf16[256,32]{0,1:T(8,128)(2,1)S(1)}, bf16[256,32]{0,1:T(8,128)(2,1)}, u32[]{:S(2)}) copy-start(bf16[256,32]{0,1:T(8,128)(2,1)} %param.8) | copy-start | bytes 49156
  33.5 3.1 %copy-start.4 = (f32[128]{0:T(128)S(1)}, f32[128]{0:T(128)}, u32[]{:S(2)}) copy-start(f32[128]{0:T(128)} %param.10) | copy-start | bytes 1540
  37.6 31.2 %all-to-all-start = ((bf16[16,4,512]{2,1,0:T(4,128)(2,1)}), bf16[16,4,512]{2,1,0:T(4,128)(2,1)}, u32[]{:S(2)}, u32[]{:S(2)}) async-start(bf16[16,4,512]{2,1,0:T(4,128)(2,1)} %all_to_all.12), calls=%async_computation | async-start | bytes 131072 | tf_op jit(solution)/shard_map/all_to_all | solution.py:96
  42.8 3.0 %copy-start.1 = (bf16[96,128]{1,0:T(8,128)(2,1)S(1)}, bf16[96,128]{1,0:T(8,128)(2,1)}, u32[]{:S(2)}) copy-start(bf16[96,128]{1,0:T(8,128)(2,1)} %reshape.54) | copy-start | bytes 73732
  70.0 3.1 %copy-start.2 = (bf16[256,32]{0,1:T(8,128)(2,1)S(1)}, bf16[256,32]{0,1:T(8,128)(2,1)}, u32[]{:S(2)}) copy-start(bf16[256,32]{0,1:T(8,128)(2,1)} %param.7) | copy-start | bytes 49156
where the time goes:
time: 74.6 us; the launch traced here: 74.2 us
  blocking collectives  46.9 us (63%)
  local copies, waits for them, and re-layouts  14.9 us (20%)
  matrix products  6.57 us (9%)
  starting transfers between devices  4.16 us (6%)
  other arithmetic  0.87 us (1%)
  between operations  0.86 us (1%)
    all_gather x1, blocking collectives, per_device(): left_segment = lax.all_gather(first_operand_rows, 'col', axis=1, tiled=True)  24.2 us
    all_gather x1, blocking collectives, per_device(): lax.all_gather(second_operand_rows, 'col', axis=1, tiled=True)  22.7 us
    convert_element_type x1, local copies, waits for them, and re-layouts, per_device(): products.astype(jnp.bfloat16)  4.19 us
    all_to_all x1, starting transfers between devices, per_device(): lax.all_to_all(stored, 'col', split_axis=0, concat_axis=1, tiled=True)  4.16 us
    reshape x2, local copies, waits for them, and re-layouts, outer_slopes(): backward.astype(jnp.bfloat16)  3.16 us
    reshape x1, local copies, waits for them, and re-layouts, per_device(): products.astype(jnp.bfloat16)  2.23 us
    dot_general x1, matrix products, per_device(): jnp.einsum('sic,sjd->ijcd', left_block, second_operand_local, preferred_e...  1.63 us
    all_to_all x2, local copies, waits for them, and re-layouts, per_device(): lax.all_to_all(stored, 'col', split_axis=0, concat_axis=1, tiled=True)  1.52 us
  transfers between devices with their start and end apart: 1, of which 0 were waited for; matrix products, arithmetic and copies ran while one was open for 6% of the time, Pallas kernels for 0%

commit v1 on v0

--- a/solution.py
+++ b/solution.py
@@ -48,7 +48,8 @@
         (alignment_row_count, local_residue_start, operand_channel_width), jnp.float32
     )
     stored = jnp.zeros((residue_total_count, local_residue_start * channels), jnp.bfloat16)
-    left_segment = lax.all_gather(first_operand_rows, "col", axis=1, tiled=True)
+    out_arr = lax.all_gather(first_operand_rows, "col")
+    left_segment = jnp.concatenate(out_arr, 1)
     right_segment = lax.all_gather(second_operand_rows, "col", axis=1, tiled=True)
     right_whole = right_segment
     piece_res = left_segment.shape[1] // operand_channel_width

time: 74.6 us -> 74.6 us (level)
  no operation moved by 1% of the time
where the time goes in v1:
time: 74.6 us; the launch traced here: 74.2 us
  blocking collectives  46.9 us (63%)
  local copies, waits for them, and re-layouts  14.9 us (20%)
  matrix products  6.57 us (9%)
  starting transfers between devices  4.16 us (6%)
  other arithmetic  0.87 us (1%)
  between operations  0.85 us (1%)
    all_gather x1, blocking collectives, per_device(): out_arr = lax.all_gather(first_operand_rows, 'col')  24.2 us
    all_gather x1, blocking collectives, per_device(): lax.all_gather(second_operand_rows, 'col', axis=1, tiled=True)  22.7 us
    convert_element_type x1, local copies, waits for them, and re-layouts, per_device(): products.astype(jnp.bfloat16)  4.19 us
    all_to_all x1, starting transfers between devices, per_device(): lax.all_to_all(stored, 'col', split_axis=0, concat_axis=1, tiled=True)  4.16 us
    reshape x2, local copies, waits for them, and re-layouts, outer_slopes(): backward.astype(jnp.bfloat16)  3.16 us
    reshape x1, local copies, waits for them, and re-layouts, per_device(): products.astype(jnp.bfloat16)  2.23 us
    dot_general x1, matrix products, per_device(): jnp.einsum('sic,sjd->ijcd', left_block, second_operand_local, preferred_e...  1.63 us
    all_to_all x2, local copies, waits for them, and re-layouts, per_device(): lax.all_to_all(stored, 'col', split_axis=0, concat_axis=1, tiled=True)  1.52 us
  transfers between devices with their start and end apart: 1, of which 0 were waited for; matrix products, arithmetic and copies ran while one was open for 6% of the time, Pallas kernels for 0%

profile of v1, /device:TPU:0, one launch (start us, length us, event | category | flops | bytes accessed | tf_op | source)
XLA Modules:
  0.0 74.2 jit_solution(1012123003351371016)
XLA Ops:
  0.6 0.0 copy-start
  0.7 1.0 %reshape.50 = bf16[384,256]{1,0:T(8,128)(2,1)S(1)} reshape(bf16[96,4,256]{2,1,0:T(4,128)(2,1)} %param.6) | data formatting | bytes 393216 | tf_op jit(solution)/shard_map/reshape | solution.py:21
  1.7 0.9 %convolution_convert_fusion = bf16[384,32]{0,1:T(8,128)(2,1)S(1)} fusion(bf16[384,256]{1,0:T(8,128)(2,1)S(1)} %reshape.50, bf16[256,32]{0,1:T(8,128)(2,1)} %param.7), kind=kOutput, calls=%fused_computation.14 | convolution fusion | flops 6303744 | bytes 237568 | tf_op jit(solution)/shard_map/dot_general | solution.py:25
  2.6 0.1 copy.31
  2.7 0.1 all_gather_reshape.3
  2.8 24.2 %all_gather.7 = bf16[16,96,128]{2,1,0:T(8,128)(2,1)S(1)} all-gather(bf16[1,96,128]{2,1,0:T(8,128)(2,1)S(1)} %all_gather_reshape.3), channel_id=1, replica_groups=mesh['group'=2,'col'=16] {'col'}, dimensions={0}, use_global_device_ids=true | all-gather | bytes 417792 | tf_op jit(solution)/shard_map/all_gather | solution.py:51
  27.0 0.3 copy.32
  27.3 0.2 convolution_convert_fusion.1
  27.5 0.1 copy.28
  27.6 1.6 %fusion = bf16[64,4,32,32]{0,3,2,1:T(8,128)(2,1)} fusion(bf16[96,64,32]{0,2,1:T(8,128)(2,1)S(1)} %bitcast.50, bf16[96,4,32,1]{2,1,0,3:T(4,128)(2,1)S(1)} %bitcast.53), kind=kOutput, calls=%fused_computation.1 | convolution fusion | flops 50855936 | bytes 942080 | tf_op jit(solution)/shard_map/sic,sjd->ijcd/dot_general | solution.py:69
  29.3 4.2 %copy.35 = bf16[64,4,32,32]{3,2,1,0:T(8,128)(2,1)S(1)} copy(bf16[64,4,32,32]{0,3,2,1:T(8,128)(2,1)} %fusion) | data formatting | bytes 1048576 | tf_op jit(solution)/shard_map/convert_element_type | solution.py:77
  33.5 2.2 %reshape.54 = bf16[256,1024]{1,0:T(8,128)(2,1)S(1)} reshape(bf16[64,4,32,32]{3,2,1,0:T(8,128)(2,1)S(1)} %copy.35) | data formatting | bytes 1048576 | tf_op jit(solution)/shard_map/reshape | solution.py:77
  35.7 0.9 %convert_multiply_fusion = f32[64,4,128]{2,1,0:T(4,128)S(1)} fusion(bf16[64,4,128]{2,1,0:T(4,128)(2,1)} %param.11), kind=kLoop, calls=%fused_computation.18 | loop fusion | flops 65536 | bytes 196608 | tf_op jit(solution)/shard_map/mul | solution.py:85
  36.6 0.3 fusion.6
  36.9 0.7 all_to_all.12
  37.6 4.2 %all-to-all-start = ((bf16[16,4,512]{2,1,0:T(4,128)(2,1)}), bf16[16,4,512]{2,1,0:T(4,128)(2,1)}, u32[]{:S(2)}, u32[]{:S(2)}) async-start(bf16[16,4,512]{2,1,0:T(4,128)(2,1)} %all_to_all.12), calls=%async_computation | async-start | bytes 131072 | tf_op jit(solution)/shard_map/all_to_all | solution.py:97
  41.7 0.7 reshape.51
  42.5 0.3 fusion.2
  42.8 1.6 %reshape.57 = bf16[64,4,32,32]{3,2,1,0:T(8,128)(2,1)S(1)} reshape(bf16[256,1024]{1,0:T(8,128)(2,1)S(1)} %fusion.2) | data formatting | bytes 1048576 | tf_op jit(solution)/shard_map/reshape | solution.py:42
  44.4 1.3 %fusion.11 = (bf16[96,4,32]{0,2,1:T(8,128)(2,1)S(1)}, f32[96,4,32]{0,2,1:T(8,128)}) fusion(bf16[96,64,32,1]{0,2,3,1:T(8,128)(2,1)S(1)} %bitcast.51, bf16[64,4,32,32]{3,2,1,0:T(8,128)(2,1)S(1)} %reshape.57), kind=kOutput, calls=%fused_computation.21 | convolution fusion | flops 50343936 | bytes 991232 | tf_op jit(solution)/shard_map/ijcd,sic->sjd/dot_general | solution.py:93
  45.7 22.7 %all_gather.6 = bf16[96,2048]{1,0:T(8,128)(2,1)S(1)} all-gather(bf16[96,128]{1,0:T(8,128)(2,1)S(1)} %copy-done.1), channel_id=1, replica_groups=mesh['group'=2,'col'=16] {'col'}, dimensions={1}, use_global_device_ids=true | all-gather | bytes 417792 | tf_op jit(solution)/shard_map/all_gather | solution.py:53
  68.4 0.3 copy.29
  68.7 0.1 copy.41
  68.8 0.9 %copy.36 = bf16[4,16,512]{2,1,0:T(8,128)(2,1)S(1)} copy(bf16[4,16,512]{2,0,1:T(4,128)(2,1)} %bitcast.9) | data formatting | bytes 131072 | tf_op jit(solution)/shard_map/all_to_all | solution.py:97
  69.7 0.1 reshape.55
  69.7 0.3 fusion.1
  70.0 1.6 %reshape.67 = bf16[4,64,32,32]{3,2,1,0:T(8,128)(2,1)S(1)} reshape(bf16[256,1024]{1,0:T(8,128)(2,1)S(1)} %fusion.1) | data formatting | bytes 1048576 | tf_op jit(solution)/shard_map/reshape | solution.py:42
  71.6 1.3 %fusion.10 = (bf16[96,4,32]{0,2,1:T(8,128)(2,1)S(1)}, f32[96,4,32]{0,2,1:T(8,128)}) fusion(bf16[96,64,32,1]{0,2,1,3:T(8,128)(2,1)S(1)} %bitcast.52, bf16[4,64,32,32]{3,2,1,0:T(8,128)(2,1)S(1)} %reshape.67), kind=kOutput, calls=%fused_computation.20 | convolution fusion | flops 50343936 | bytes 991232 | tf_op jit(solution)/shard_map/ijcd,sjd->sic/dot_general | solution.py:111
  73.0 0.1 copy.40
  73.1 0.2 fusion.12
  73.3 0.2 fusion.3
  73.5 0.7 reshape.60
  (10 shorter events, 0.0 us)
Async XLA Ops:
  0.6 36.0 %copy-start = (bf16[1024,128]{1,0:T(8,128)(2,1)S(1)}, bf16[1024,128]{1,0:T(8,128)(2,1)}, u32[]{:S(2)}) copy-start(bf16[1024,128]{1,0:T(8,128)(2,1)} %param.9) | copy-start | bytes 786436
  0.6 26.7 %copy-start.3 = (bf16[256,32]{0,1:T(8,128)(2,1)S(1)}, bf16[256,32]{0,1:T(8,128)(2,1)}, u32[]{:S(2)}) copy-start(bf16[256,32]{0,1:T(8,128)(2,1)} %param.8) | copy-start | bytes 49156
  33.5 3.1 %copy-start.4 = (f32[128]{0:T(128)S(1)}, f32[128]{0:T(128)}, u32[]{:S(2)}) copy-start(f32[128]{0:T(128)} %param.10) | copy-start | bytes 1540
  37.6 31.2 %all-to-all-start = ((bf16[16,4,512]{2,1,0:T(4,128)(2,1)}), bf16[16,4,512]{2,1,0:T(4,128)(2,1)}, u32[]{:S(2)}, u32[]{:S(2)}) async-start(bf16[16,4,512]{2,1,0:T(4,128)(2,1)} %all_to_all.12), calls=%async_computation | async-start | bytes 131072 | tf_op jit(solution)/shard_map/all_to_all | solution.py:97
  42.8 3.0 %copy-start.1 = (bf16[96,128]{1,0:T(8,128)(2,1)S(1)}, bf16[96,128]{1,0:T(8,128)(2,1)}, u32[]{:S(2)}) copy-start(bf16[96,128]{1,0:T(8,128)(2,1)} %reshape.51) | copy-start | bytes 73732
  70.0 3.1 %copy-start.2 = (bf16[256,32]{0,1:T(8,128)(2,1)S(1)}, bf16[256,32]{0,1:T(8,128)(2,1)}, u32[]{:S(2)}) copy-start(bf16[256,32]{0,1:T(8,128)(2,1)} %param.7) | copy-start | bytes 49156
